TPU v7x, 32 devices: a whole 2x2x4 slice. The times are simulated.
32 devices in a mesh: lat: 4 (over z), lon: 8 (over y, x, core).
Axes of the slice: x: 2, y: 2, z: 4, core: 2. Of those that a mesh axis runs over, the one named last changes fastest.
Arguments:
- lat_coef: float32 [4, 256, 1024], P(None, 'lat', 'lon'), may hold values from 0.02 to 0.12
- lon_coef: float32 [4, 256, 1024], P(None, 'lat', 'lon'), may hold values from 0.02 to 0.12
- std_scale: float32 [4, 256, 1024], P(None, 'lat', 'lon'), may hold values from 0.5 to 2
- land_mask: int32 [256, 1024], P('lat', 'lon'), may hold values 0 or 1
- lst_weights: float32 [4], replicated, may hold values from 0.1 to 0.6
- innovation: float32 [16384, 128], P(('lat', 'lon')), may hold values from -6 to 6
- inv_var: float32 [16384, 128], P(('lat', 'lon')), may hold values from 0.2 to 5
- owner: int32 [16384, 1], P(('lat', 'lon')), may hold values from 0 to 31; in each aligned block of 512 rows (0 to 511, 512 to 1023, ...) at most 32 rows name the same one
- row_ids: int32 [16384], P(('lat', 'lon')), may hold values from 0 to 63
- offsets: int32 [16384, 128], P(('lat', 'lon')), may hold values from 0 to 127
Outputs:
- increment: float32 [4, 256, 1024], P(None, 'lat', 'lon')
- departure: float32 [16384, 128], P(('lat', 'lon'))
Inputs may be any that keep to these rules, and one draw needn't show every extreme that they name: Within the 512 tiles of one device no owner is named more than 32 times.
All inputs are finite; a program needn't handle non-finite values. No bound on the sum of `land_mask` on one device may be relied on, other than what follows from the above.
Results may differ from a plain program's by a relative error of at most 0.00026.
Values sent between devices are 32-bit elements; how exact they have to be, the bound alone decides.
No kernel may reach another device: no remote copies, remote signals or barrier semaphores. Data moves between devices by JAX's collectives and lax.ppermute only.
A program may use at most 64 MiB of HBM per device.

v0:
```python
import math
import jax
import jax.numpy as jnp
from jax import lax
from jax.sharding import PartitionSpec as P

PASSES = 8
ITERS = 2


def with_halo(block, sides, width, periodic):
    for axis, dim in sides:
        count = lax.axis_size(axis)
        forward = [(i, i + 1) for i in range(count - 1)]
        if periodic:
            forward.append((count - 1, 0))
        backward = [(target, source) for source, target in forward]
        low = lax.ppermute(
            lax.slice_in_dim(block, block.shape[dim] - width, None, axis=dim), axis, forward
        )
        high = lax.ppermute(lax.slice_in_dim(block, 0, width, axis=dim), axis, backward)
        block = jnp.concatenate([low, block, high], axis=dim)
    return block


def lst_of(weights, field):
    total = weights[0] * field[0]
    for index in range(1, field.shape[0]):
        total = total + weights[index] * field[index]
    return total


def extend(field, width):
    taller = with_halo(field, (("lat", 1),), width, False)
    return with_halo(taller, (("lon", 2),), width, True)


def pass_step(field, north_face, east_face):
    centre = field[:, 1:-1, 1:-1]
    north = field[:, 2:, 1:-1]
    south = field[:, :-2, 1:-1]
    east = field[:, 1:-1, 2:]
    west = field[:, 1:-1, :-2]
    face_north = north_face[:, 1:-1, 1:-1]
    face_south = north_face[:, :-2, 1:-1]
    face_east = east_face[:, 1:-1, 1:-1]
    face_west = east_face[:, 1:-1, :-2]
    return (
        centre
        + face_north * (north - centre)
        - face_south * (centre - south)
        + face_east * (east - centre)
        - face_west * (centre - west)
    )


def diffuse(field, faces, rim_depth):
    fields = field.shape[0]
    for block in range(PASSES // rim_depth):
        grown = extend(field, rim_depth)
        for inner in range(rim_depth):
            window = faces[:, inner : faces.shape[1] - inner, inner : faces.shape[2] - inner]
            grown = pass_step(grown, window[:fields], window[fields:])
        field = grown
    return field


def total_sum(value):
    return lax.psum(value, ("lat", "lon"))


def cells_to_rows(values, offsets):
    columns = lax.broadcasted_iota(jnp.int32, (1, 1, offsets.shape[1]), 2)
    return jnp.sum(jnp.where(offsets[:, :, None] == columns, values[:, :, None], 0.0), axis=1)


def rows_to_cells(rows, offsets):
    columns = lax.broadcasted_iota(jnp.int32, (1, 1, offsets.shape[1]), 2)
    return jnp.sum(jnp.where(offsets[:, :, None] == columns, rows[:, None, :], 0.0), axis=2)


def blockwise(func, first, offsets):
    count, width = first.shape
    block_rows = math.gcd(count, 64)
    shaped = (count // block_rows, block_rows, width)

    def apply_block(pair):
        return func(pair[0], pair[1])

    result = lax.map(apply_block, (first.reshape(shaped), offsets.reshape(shaped)))
    return result.reshape(count, width)


def contract_first(left, right):
    return lax.dot_general(
        left,
        right,
        (((0,), (0,)), ((), ())),
        precision=lax.Precision.HIGHEST,
        preferred_element_type=jnp.float32,
    )


def on_device(
    lat_coef,
    lon_coef,
    std_scale,
    land_mask,
    lst_weights,
    innovation,
    inv_var,
    owner,
    row_ids,
    offsets,
):
    fields, tile_rows, tile_cols = lat_coef.shape
    tiles_here, row_width = innovation.shape
    devices = lax.axis_size("lat") * lax.axis_size("lon")
    capacity = max(2, 2 * tiles_here // devices)
    rows_here = tile_rows * tile_cols // row_width
    global_row = lax.axis_index("lat") * tile_rows + lax.broadcasted_iota(
        jnp.int32, (1, tile_rows, 1), 1
    )
    north_face = jnp.where(global_row == lax.axis_size("lat") * tile_rows - 1, 0.0, lat_coef)
    rim_depth = 4
    faces = extend(jnp.concatenate([north_face, lon_coef], 0), rim_depth)
    mask_field = land_mask.astype(jnp.float32)

    def forward(vector):
        return mask_field * std_scale * diffuse(vector, faces, rim_depth)

    def adjoint(vector):
        return diffuse(mask_field * std_scale * vector, faces, rim_depth)

    def spread(grid):
        return lst_weights[:, None, None] * grid[None]

    destination = owner[:, 0]
    hits = (destination[:, None] == jnp.arange(devices, dtype=jnp.int32)[None, :]).astype(jnp.int32)
    bucket_rank = jnp.sum(jnp.cumsum(hits, axis=0) * hits, axis=1) - 1
    slot_index = destination * capacity + bucket_rank
    slot_range = jnp.arange(devices * capacity, dtype=jnp.int32)
    placement = (slot_range[:, None] == slot_index[None, :]).astype(jnp.float32)
    send_ids = (
        jnp.sum(
            jnp.where(slot_range[:, None] == slot_index[None, :], row_ids[None, :] + 1, 0), axis=1
        )
        - 1
    )
    got_ids = lax.all_to_all(send_ids, ("lat", "lon"), split_axis=0, concat_axis=0, tiled=True)
    ownership = (got_ids[:, None] == jnp.arange(rows_here, dtype=jnp.int32)[None, :]).astype(
        jnp.float32
    )

    def to_rows(values):
        return blockwise(cells_to_rows, values, offsets)

    def pack(rows):
        return jnp.dot(
            placement, rows, precision=lax.Precision.HIGHEST, preferred_element_type=jnp.float32
        )

    def collect(buffer):
        return contract_first(ownership, buffer)

    def send_back(values):
        arrived = lax.all_to_all(
            pack(to_rows(values)), ("lat", "lon"), split_axis=0, concat_axis=0, tiled=True
        )
        return spread(collect(arrived))

    residual = adjoint(send_back(inv_var * innovation))
    direction = residual
    norm_now = total_sum(jnp.sum(residual * residual))
    increment = jnp.zeros_like(residual)
    analysed = jnp.zeros_like(innovation)
    for index in range(ITERS):
        image = forward(direction)
        returned = lax.all_to_all(
            jnp.dot(
                ownership,
                lst_of(lst_weights, image),
                precision=lax.Precision.HIGHEST,
                preferred_element_type=jnp.float32,
            ),
            ("lat", "lon"),
            split_axis=0,
            concat_axis=0,
            tiled=True,
        )
        seen = blockwise(rows_to_cells, contract_first(placement, returned), offsets)
        product = direction + adjoint(send_back(inv_var * seen))
        step_size = norm_now / total_sum(jnp.sum(direction * product))
        increment = increment + step_size * image
        analysed = analysed + step_size * seen
        if index + 1 < ITERS:
            residual = residual - step_size * product
            norm_next = total_sum(jnp.sum(residual * residual))
            direction = residual + norm_next / norm_now * direction
            norm_now = norm_next
    return (increment, innovation - analysed)


def solution(mesh):
    in_specs = (
        P(None, "lat", "lon"),
        P(None, "lat", "lon"),
        P(None, "lat", "lon"),
        P("lat", "lon"),
        P(),
        P(("lat", "lon"), None),
        P(("lat", "lon"), None),
        P(("lat", "lon"), None),
        P(("lat", "lon")),
        P(("lat", "lon"), None),
    )
    out_specs = (P(None, "lat", "lon"), P(("lat", "lon"), None))
    return jax.shard_map(
        on_device, mesh=mesh, in_specs=in_specs, out_specs=out_specs, check_vma=False
    )
```

profile of v0, /device:TPU:0, one launch (start us, length us, event | category | flops | bytes accessed | tf_op | source)
XLA Modules:
  0.0 555.1 jit_solution(16266994151909909597)
XLA Ops:
  5.3 7.3 %all-to-all-start = ((s32[32,32,1]{1,2,0:T(1,128)}), s32[32,32,1]{1,2,0:T(1,128)S(1)}, u32[]{:S(2)}, u32[]{:S(2)}) async-start(s32[32,32,1]{1,2,0:T(1,128)} %sub.738), calls=%async_computation | async-start | bytes 32768 | tf_op jit(solution)/shard_map/all_to_all | solution.py:150
  13.7 22.9 %while.50 = (s32[]{:T(128)}, f32[8,64,128]{2,1,0:T(8,128)S(1)}, s32[8,64,128]{2,1,0:T(8,128)S(1)}, f32[8,64,128]{2,1,0:T(8,128)S(1)}, s32[]{:T(128)}) while((s32[]{:T(128)}, f32[8,64,128]{2,1,0:T(8,128)S(1)}, s32[8,64,128]{2,1,0:T(8,128)S(1)}, f32[8,64,128]{2,1,0:T(8,128)S(1)}, s32[]{:T(128)}) %tuple.124), condition=%wide.region_6.7_spmd, body=%wide.region_4.6_spmd.sunk | while | flops 3137538 | bytes 294985 | solution.py:90
  38.5 5.8 %all-to-all-start.1 = ((f32[32,32,128]{2,1,0:T(8,128)}), f32[32,32,128]{2,1,0:T(8,128)S(1)}, u32[]{:S(2)}, u32[]{:S(2)}) async-start(f32[32,32,128]{2,1,0:T(8,128)} %fusion.4), calls=%async_computation.1 | async-start | bytes 1048576 | tf_op jit(solution)/shard_map/all_to_all | solution.py:167
  60.8 5.1 collective-permute-start
  67.5 4.0 collective-permute-done.1
  83.7 4.2 collective-permute-done.9
  90.8 4.4 collective-permute-done.10
  100.8 4.2 collective-permute-done.13
  117.3 4.2 collective-permute-done.17
  136.9 15.2 %all-to-all-done.2 = f32[32,32,128]{2,1,0:T(8,128)S(1)} async-done(((f32[32,32,128]{2,1,0:T(8,128)}), f32[32,32,128]{2,1,0:T(8,128)S(1)}, u32[]{:S(2)}, u32[]{:S(2)}) %all-to-all-start.2) | async-done | bytes 524320 | tf_op jit(solution)/shard_map/all_to_all | solution.py:179
  153.9 27.1 %while.51 = (s32[]{:T(128)}, f32[8,64,128]{2,1,0:T(8,128)S(1)}, s32[8,64,128]{2,1,0:T(8,128)S(1)}, f32[8,64,128]{2,1,0:T(8,128)}, s32[]{:T(128)}) while((s32[]{:T(128)}, f32[8,64,128]{2,1,0:T(8,128)S(1)}, s32[8,64,128]{2,1,0:T(8,128)S(1)}, f32[8,64,128]{2,1,0:T(8,128)}, s32[]{:T(128)}) %tuple.119), condition=%wide.region_11.12_spmd, body=%wide.region_9.11_spmd.sunk | while | flops 3137538 | bytes 294985 | solution.py:90
  181.7 27.3 %while.52 = (s32[]{:T(128)}, f32[8,64,128]{2,1,0:T(8,128)}, s32[8,64,128]{2,1,0:T(8,128)S(1)}, f32[8,64,128]{2,1,0:T(8,128)S(1)}, s32[]{:T(128)}) while((s32[]{:T(128)}, f32[8,64,128]{2,1,0:T(8,128)}, s32[8,64,128]{2,1,0:T(8,128)S(1)}, f32[8,64,128]{2,1,0:T(8,128)S(1)}, s32[]{:T(128)}) %tuple.125), condition=%wide.region_14.15_spmd, body=%wide.region_12.14_spmd.sunk | while | flops 3137538 | bytes 295493 | solution.py:90
  211.1 18.4 %all_to_all.54 = f32[32,32,128]{2,1,0:T(8,128)S(1)} all-to-all(f32[32,32,128]{2,1,0:T(8,128)S(1)} %fusion.2), channel_id=1, replica_groups=mesh['lat'=4,'lon'=8] {'lat','lon'}, dimensions={0} | all-to-all | bytes 1048576 | tf_op jit(solution)/shard_map/all_to_all | solution.py:167
  234.8 4.2 collective-permute-done.21
  242.0 4.0 collective-permute-done.22
  251.3 4.2 collective-permute-done.25
  258.3 4.0 collective-permute-done.26
  265.3 38.2 %all-reduce = (f32[]{:T(128)}, f32[]{:T(128)}) all-reduce(f32[]{:T(128)} %get-tuple-element.118, f32[]{:T(128)} %get-tuple-element.117), channel_id=1, replica_groups=mesh['lat'=4,'lon'=8] {'lat','lon'}, use_global_device_ids=true, to_apply=%region_8.9 | all-reduce | flops 2 | bytes 16 | tf_op jit(solution)/shard_map/psum | solution.py:69
  305.5 40.8 %psum.30 = f32[]{:T(128)} all-reduce(f32[]{:T(128)} %multiply_reduce_fusion), channel_id=1, replica_groups=mesh['lat'=4,'lon'=8] {'lat','lon'}, use_global_device_ids=true, to_apply=%region_18.19 | all-reduce | flops 1 | bytes 8 | tf_op jit(solution)/shard_map/psum | solution.py:69
  352.5 4.2 collective-permute-done.29
  369.1 4.2 collective-permute-done.33
  376.3 3.9 collective-permute-done.34
  382.6 3.7 fusion.16
  390.0 15.6 %all-to-all-done.4 = f32[32,32,128]{2,1,0:T(8,128)} async-done(((f32[32,32,128]{2,1,0:T(8,128)}), f32[32,32,128]{2,1,0:T(8,128)}, u32[]{:S(2)}, u32[]{:S(2)}) %all-to-all-start.4) | async-done | bytes 524320 | tf_op jit(solution)/shard_map/all_to_all | solution.py:179
  408.3 27.1 %while.53 = (s32[]{:T(128)}, f32[8,64,128]{2,1,0:T(8,128)S(1)}, s32[8,64,128]{2,1,0:T(8,128)S(1)}, f32[8,64,128]{2,1,0:T(8,128)}, s32[]{:T(128)}) while((s32[]{:T(128)}, f32[8,64,128]{2,1,0:T(8,128)S(1)}, s32[8,64,128]{2,1,0:T(8,128)S(1)}, f32[8,64,128]{2,1,0:T(8,128)}, s32[]{:T(128)}) %tuple.121), condition=%wide.region_21.22_spmd, body=%wide.region_19.21_spmd.sunk | while | flops 3137538 | bytes 294985 | solution.py:90
  435.4 22.9 %while.54 = (s32[]{:T(128)}, f32[8,64,128]{2,1,0:T(8,128)S(1)}, s32[8,64,128]{2,1,0:T(8,128)S(1)}, f32[8,64,128]{2,1,0:T(8,128)S(1)}, s32[]{:T(128)}) while((s32[]{:T(128)}, f32[8,64,128]{2,1,0:T(8,128)S(1)}, s32[8,64,128]{2,1,0:T(8,128)S(1)}, f32[8,64,128]{2,1,0:T(8,128)S(1)}, s32[]{:T(128)}) %tuple.123), condition=%wide.region_24.25_spmd, body=%wide.region_22.24_spmd.sunk | while | flops 3137538 | bytes 294985 | solution.py:90
  459.4 18.4 %all_to_all.55 = f32[32,32,128]{2,1,0:T(8,128)S(1)} all-to-all(f32[32,32,128]{2,1,0:T(8,128)S(1)} %fusion), channel_id=1, replica_groups=mesh['lat'=4,'lon'=8] {'lat','lon'}, dimensions={0} | all-to-all | bytes 1048576 | tf_op jit(solution)/shard_map/all_to_all | solution.py:167
  483.1 4.2 collective-permute-done.37
  490.1 4.3 collective-permute-done.38
  499.8 4.2 collective-permute-done.41
  507.0 3.8 collective-permute-done.42
  513.8 38.2 %psum.31 = f32[]{:T(128)} all-reduce(f32[]{:T(128)} %fusion.267), channel_id=1, replica_groups=mesh['lat'=4,'lon'=8] {'lat','lon'}, use_global_device_ids=true, to_apply=%region_26.27 | all-reduce | flops 1 | bytes 8 | tf_op jit(solution)/shard_map/psum | solution.py:69
  (383 shorter events, 274.9 us)
Async XLA Ops:
  5.3 33.1 %all-to-all-start = ((s32[32,32,1]{1,2,0:T(1,128)}), s32[32,32,1]{1,2,0:T(1,128)S(1)}, u32[]{:S(2)}, u32[]{:S(2)}) async-start(s32[32,32,1]{1,2,0:T(1,128)} %sub.738), calls=%async_computation | async-start | bytes 32768 | tf_op jit(solution)/shard_map/all_to_all | solution.py:150
  38.5 21.5 %all-to-all-start.1 = ((f32[32,32,128]{2,1,0:T(8,128)}), f32[32,32,128]{2,1,0:T(8,128)S(1)}, u32[]{:S(2)}, u32[]{:S(2)}) async-start(f32[32,32,128]{2,1,0:T(8,128)} %fusion.4), calls=%async_computation.1 | async-start | bytes 1048576 | tf_op jit(solution)/shard_map/all_to_all | solution.py:167
  44.4 9.4 %collective-permute-start.4 = (f32[8,4,128]{2,1,0:T(4,128)S(1)}, f32[8,4,128]{2,1,0:T(4,128)S(1)}, u32[]{:S(2)}, u32[]{:S(2)}) collective-permute-start(f32[8,4,128]{2,1,0:T(4,128)S(1)} %get-tuple-element.166), channel_id=1, source_target_pairs={{0,8},{8,16},{16,24},{1,9},{9,17},{17,25},{2,10},{10,18},{18,26},{... | collective-permute-start | bytes 49160 | tf_op jit(solution)/shard_map/ppermute | solution.py:18
  48.1 5.8 %collective-permute-start.5 = (f32[8,4,128]{2,1,0:T(4,128)S(1)}, f32[8,4,128]{2,1,0:T(4,128)S(1)}, u32[]{:S(2)}, u32[]{:S(2)}) collective-permute-start(f32[8,4,128]{2,1,0:T(4,128)S(1)} %get-tuple-element.167), channel_id=1, source_target_pairs={{8,0},{16,8},{24,16},{9,1},{17,9},{25,17},{10,2},{18,10},{26,18},{... | collective-permute-start | bytes 49160 | tf_op jit(solution)/shard_map/ppermute | solution.py:21
  54.1 13.1 %collective-permute-start.6 = (f32[8,72,4]{2,1,0:T(8,128)S(1)}, f32[8,72,4]{2,1,0:T(8,128)S(1)}, u32[]{:S(2)}, u32[]{:S(2)}) collective-permute-start(f32[8,72,4]{2,1,0:T(8,128)S(1)} %get-tuple-element.164), channel_id=1, source_target_pairs={{0,1},{1,2},{2,3},{3,4},{4,5},{5,6},{6,7},{7,0},{8,9},{9,10},{10,1... | collective-permute-start | bytes 27656 | tf_op jit(solution)/shard_map/ppermute | solution.py:18
  54.2 20.1 %collective-permute-start.7 = (f32[8,72,4]{2,1,0:T(8,128)S(1)}, f32[8,72,4]{2,1,0:T(8,128)}, u32[]{:S(2)}, u32[]{:S(2)}) collective-permute-start(f32[8,72,4]{2,1,0:T(8,128)S(1)} %get-tuple-element.165), channel_id=1, source_target_pairs={{1,0},{2,1},{3,2},{4,3},{5,4},{6,5},{7,6},{0,7},{9,8},{10,9},{11,1... | collective-permute-start | bytes 27656 | tf_op jit(solution)/shard_map/ppermute | solution.py:21
  60.8 6.7 %collective-permute-start = (f32[4,4,128]{2,1,0:T(4,128)S(1)}, f32[4,4,128]{2,1,0:T(4,128)S(1)}, u32[]{:S(2)}, u32[]{:S(2)}) collective-permute-start(f32[4,4,128]{2,1,0:T(4,128)S(1)} %get-tuple-element.206), channel_id=1, source_target_pairs={{0,8},{8,16},{16,24},{1,9},{9,17},{17,25},{2,10},{10,18},{18,26},{... | collective-permute-start | bytes 24584 | tf_op jit(solution)/shard_map/ppermute | solution.py:18
  65.9 5.5 collective-permute-start.1
  71.5 6.2 %collective-permute-start.2 = (f32[4,72,4]{2,1,0:T(8,128)S(1)}, f32[4,72,4]{2,1,0:T(8,128)S(1)}, u32[]{:S(2)}, u32[]{:S(2)}) collective-permute-start(f32[4,72,4]{2,1,0:T(8,128)S(1)} %get-tuple-element.186), channel_id=1, source_target_pairs={{0,1},{1,2},{2,3},{3,4},{4,5},{5,6},{6,7},{7,0},{8,9},{9,10},{10,1... | collective-permute-start | bytes 13832 | tf_op jit(solution)/shard_map/ppermute | solution.py:18
  71.6 6.1 %collective-permute-start.3 = (f32[4,72,4]{2,1,0:T(8,128)S(1)}, f32[4,72,4]{2,1,0:T(8,128)S(1)}, u32[]{:S(2)}, u32[]{:S(2)}) collective-permute-start(f32[4,72,4]{2,1,0:T(8,128)S(1)} %get-tuple-element.187), channel_id=1, source_target_pairs={{1,0},{2,1},{3,2},{4,3},{5,4},{6,5},{7,6},{0,7},{9,8},{10,9},{11,1... | collective-permute-start | bytes 13832 | tf_op jit(solution)/shard_map/ppermute | solution.py:21
  82.4 5.5 collective-permute-start.9
  88.1 7.1 %collective-permute-start.10 = (f32[4,72,4]{2,1,0:T(8,128)S(1)}, f32[4,72,4]{2,1,0:T(8,128)S(1)}, u32[]{:S(2)}, u32[]{:S(2)}) collective-permute-start(f32[4,72,4]{2,1,0:T(8,128)S(1)} %get-tuple-element.184), channel_id=1, source_target_pairs={{0,1},{1,2},{2,3},{3,4},{4,5},{5,6},{6,7},{7,0},{8,9},{9,10},{10,1... | collective-permute-start | bytes 13832 | tf_op jit(solution)/shard_map/ppermute | solution.py:18
  88.1 7.0 %collective-permute-start.11 = (f32[4,72,4]{2,1,0:T(8,128)S(1)}, f32[4,72,4]{2,1,0:T(8,128)S(1)}, u32[]{:S(2)}, u32[]{:S(2)}) collective-permute-start(f32[4,72,4]{2,1,0:T(8,128)S(1)} %get-tuple-element.185), channel_id=1, source_target_pairs={{1,0},{2,1},{3,2},{4,3},{5,4},{6,5},{7,6},{0,7},{9,8},{10,9},{11,1... | collective-permute-start | bytes 13832 | tf_op jit(solution)/shard_map/ppermute | solution.py:21
  105.2 6.4 %collective-permute-start.14 = (f32[4,72,4]{2,1,0:T(8,128)S(1)}, f32[4,72,4]{2,1,0:T(8,128)S(1)}, u32[]{:S(2)}, u32[]{:S(2)}) collective-permute-start(f32[4,72,4]{2,1,0:T(8,128)S(1)} %get-tuple-element.182), channel_id=1, source_target_pairs={{0,1},{1,2},{2,3},{3,4},{4,5},{5,6},{6,7},{7,0},{8,9},{9,10},{10,1... | collective-permute-start | bytes 13832 | tf_op jit(solution)/shard_map/ppermute | solution.py:18
  105.2 6.4 %collective-permute-start.15 = (f32[4,72,4]{2,1,0:T(8,128)S(1)}, f32[4,72,4]{2,1,0:T(8,128)S(1)}, u32[]{:S(2)}, u32[]{:S(2)}) collective-permute-start(f32[4,72,4]{2,1,0:T(8,128)S(1)} %get-tuple-element.183), channel_id=1, source_target_pairs={{1,0},{2,1},{3,2},{4,3},{5,4},{6,5},{7,6},{0,7},{9,8},{10,9},{11,1... | collective-permute-start | bytes 13832 | tf_op jit(solution)/shard_map/ppermute | solution.py:21
  115.9 5.5 collective-permute-start.17
  121.6 5.9 %collective-permute-start.18 = (f32[4,72,4]{2,1,0:T(8,128)S(1)}, f32[4,72,4]{2,1,0:T(8,128)S(1)}, u32[]{:S(2)}, u32[]{:S(2)}) collective-permute-start(f32[4,72,4]{2,1,0:T(8,128)S(1)} %get-tuple-element.180), channel_id=1, source_target_pairs={{0,1},{1,2},{2,3},{3,4},{4,5},{5,6},{6,7},{7,0},{8,9},{9,10},{10,1... | collective-permute-start | bytes 13832 | tf_op jit(solution)/shard_map/ppermute | solution.py:18
  121.7 5.9 %collective-permute-start.19 = (f32[4,72,4]{2,1,0:T(8,128)S(1)}, f32[4,72,4]{2,1,0:T(8,128)S(1)}, u32[]{:S(2)}, u32[]{:S(2)}) collective-permute-start(f32[4,72,4]{2,1,0:T(8,128)S(1)} %get-tuple-element.181), channel_id=1, source_target_pairs={{1,0},{2,1},{3,2},{4,3},{5,4},{6,5},{7,6},{0,7},{9,8},{10,9},{11,1... | collective-permute-start | bytes 13832 | tf_op jit(solution)/shard_map/ppermute | solution.py:21
  133.6 18.5 %all-to-all-start.2 = ((f32[32,32,128]{2,1,0:T(8,128)}), f32[32,32,128]{2,1,0:T(8,128)S(1)}, u32[]{:S(2)}, u32[]{:S(2)}) async-start(f32[32,32,128]{2,1,0:T(8,128)} %fusion.18), calls=%async_computation.2 | async-start | bytes 1048576 | tf_op jit(solution)/shard_map/all_to_all | solution.py:179
  239.1 6.8 %collective-permute-start.22 = (f32[4,72,4]{2,1,0:T(8,128)S(1)}, f32[4,72,4]{2,1,0:T(8,128)S(1)}, u32[]{:S(2)}, u32[]{:S(2)}) collective-permute-start(f32[4,72,4]{2,1,0:T(8,128)S(1)} %get-tuple-element.178), channel_id=1, source_target_pairs={{0,1},{1,2},{2,3},{3,4},{4,5},{5,6},{6,7},{7,0},{8,9},{9,10},{10,1... | collective-permute-start | bytes 13832 | tf_op jit(solution)/shard_map/ppermute | solution.py:18
  239.2 6.8 %collective-permute-start.23 = (f32[4,72,4]{2,1,0:T(8,128)S(1)}, f32[4,72,4]{2,1,0:T(8,128)S(1)}, u32[]{:S(2)}, u32[]{:S(2)}) collective-permute-start(f32[4,72,4]{2,1,0:T(8,128)S(1)} %get-tuple-element.179), channel_id=1, source_target_pairs={{1,0},{2,1},{3,2},{4,3},{5,4},{6,5},{7,6},{0,7},{9,8},{10,9},{11,1... | collective-permute-start | bytes 13832 | tf_op jit(solution)/shard_map/ppermute | solution.py:21
  255.6 6.7 %collective-permute-start.26 = (f32[4,72,4]{2,1,0:T(8,128)S(1)}, f32[4,72,4]{2,1,0:T(8,128)S(1)}, u32[]{:S(2)}, u32[]{:S(2)}) collective-permute-start(f32[4,72,4]{2,1,0:T(8,128)S(1)} %get-tuple-element.176), channel_id=1, source_target_pairs={{0,1},{1,2},{2,3},{3,4},{4,5},{5,6},{6,7},{7,0},{8,9},{9,10},{10,1... | collective-permute-start | bytes 13832 | tf_op jit(solution)/shard_map/ppermute | solution.py:18
  255.7 6.6 %collective-permute-start.27 = (f32[4,72,4]{2,1,0:T(8,128)S(1)}, f32[4,72,4]{2,1,0:T(8,128)S(1)}, u32[]{:S(2)}, u32[]{:S(2)}) collective-permute-start(f32[4,72,4]{2,1,0:T(8,128)S(1)} %get-tuple-element.177), channel_id=1, source_target_pairs={{1,0},{2,1},{3,2},{4,3},{5,4},{6,5},{7,6},{0,7},{9,8},{10,9},{11,1... | collective-permute-start | bytes 13832 | tf_op jit(solution)/shard_map/ppermute | solution.py:21
  356.8 5.6 %collective-permute-start.30 = (f32[4,72,4]{2,1,0:T(8,128)S(1)}, f32[4,72,4]{2,1,0:T(8,128)S(1)}, u32[]{:S(2)}, u32[]{:S(2)}) collective-permute-start(f32[4,72,4]{2,1,0:T(8,128)S(1)} %get-tuple-element.174), channel_id=1, source_target_pairs={{0,1},{1,2},{2,3},{3,4},{4,5},{5,6},{6,7},{7,0},{8,9},{9,10},{10,1... | collective-permute-start | bytes 13832 | tf_op jit(solution)/shard_map/ppermute | solution.py:18
  356.9 5.9 %collective-permute-start.31 = (f32[4,72,4]{2,1,0:T(8,128)S(1)}, f32[4,72,4]{2,1,0:T(8,128)S(1)}, u32[]{:S(2)}, u32[]{:S(2)}) collective-permute-start(f32[4,72,4]{2,1,0:T(8,128)S(1)} %get-tuple-element.175), channel_id=1, source_target_pairs={{1,0},{2,1},{3,2},{4,3},{5,4},{6,5},{7,6},{0,7},{9,8},{10,9},{11,1... | collective-permute-start | bytes 13832 | tf_op jit(solution)/shard_map/ppermute | solution.py:21
  373.4 6.8 %collective-permute-start.34 = (f32[4,72,4]{2,1,0:T(8,128)S(1)}, f32[4,72,4]{2,1,0:T(8,128)S(1)}, u32[]{:S(2)}, u32[]{:S(2)}) collective-permute-start(f32[4,72,4]{2,1,0:T(8,128)S(1)} %get-tuple-element.172), channel_id=1, source_target_pairs={{0,1},{1,2},{2,3},{3,4},{4,5},{5,6},{6,7},{7,0},{8,9},{9,10},{10,1... | collective-permute-start | bytes 13832 | tf_op jit(solution)/shard_map/ppermute | solution.py:18
  374.1 6.2 %collective-permute-start.35 = (f32[4,72,4]{2,1,0:T(8,128)S(1)}, f32[4,72,4]{2,1,0:T(8,128)S(1)}, u32[]{:S(2)}, u32[]{:S(2)}) collective-permute-start(f32[4,72,4]{2,1,0:T(8,128)S(1)} %get-tuple-element.173), channel_id=1, source_target_pairs={{1,0},{2,1},{3,2},{4,3},{5,4},{6,5},{7,6},{0,7},{9,8},{10,9},{11,1... | collective-permute-start | bytes 13832 | tf_op jit(solution)/shard_map/ppermute | solution.py:21
  386.3 19.2 %all-to-all-start.4 = ((f32[32,32,128]{2,1,0:T(8,128)}), f32[32,32,128]{2,1,0:T(8,128)}, u32[]{:S(2)}, u32[]{:S(2)}) async-start(f32[32,32,128]{2,1,0:T(8,128)} %fusion.16), calls=%async_computation.4 | async-start | bytes 1048576 | tf_op jit(solution)/shard_map/all_to_all | solution.py:179
  487.4 7.0 %collective-permute-start.38 = (f32[4,72,4]{2,1,0:T(8,128)S(1)}, f32[4,72,4]{2,1,0:T(8,128)S(1)}, u32[]{:S(2)}, u32[]{:S(2)}) collective-permute-start(f32[4,72,4]{2,1,0:T(8,128)S(1)} %get-tuple-element.170), channel_id=1, source_target_pairs={{0,1},{1,2},{2,3},{3,4},{4,5},{5,6},{6,7},{7,0},{8,9},{9,10},{10,1... | collective-permute-start | bytes 13832 | tf_op jit(solution)/shard_map/ppermute | solution.py:18
  487.5 6.9 %collective-permute-start.39 = (f32[4,72,4]{2,1,0:T(8,128)S(1)}, f32[4,72,4]{2,1,0:T(8,128)S(1)}, u32[]{:S(2)}, u32[]{:S(2)}) collective-permute-start(f32[4,72,4]{2,1,0:T(8,128)S(1)} %get-tuple-element.171), channel_id=1, source_target_pairs={{1,0},{2,1},{3,2},{4,3},{5,4},{6,5},{7,6},{0,7},{9,8},{10,9},{11,1... | collective-permute-start | bytes 13832 | tf_op jit(solution)/shard_map/ppermute | solution.py:21
  504.1 6.7 %collective-permute-start.42 = (f32[4,72,4]{2,1,0:T(8,128)S(1)}, f32[4,72,4]{2,1,0:T(8,128)S(1)}, u32[]{:S(2)}, u32[]{:S(2)}) collective-permute-start(f32[4,72,4]{2,1,0:T(8,128)S(1)} %get-tuple-element.168), channel_id=1, source_target_pairs={{0,1},{1,2},{2,3},{3,4},{4,5},{5,6},{6,7},{7,0},{8,9},{9,10},{10,1... | collective-permute-start | bytes 13832 | tf_op jit(solution)/shard_map/ppermute | solution.py:18
  504.1 6.7 %collective-permute-start.43 = (f32[4,72,4]{2,1,0:T(8,128)S(1)}, f32[4,72,4]{2,1,0:T(8,128)S(1)}, u32[]{:S(2)}, u32[]{:S(2)}) collective-permute-start(f32[4,72,4]{2,1,0:T(8,128)S(1)} %get-tuple-element.169), channel_id=1, source_target_pairs={{1,0},{2,1},{3,2},{4,3},{5,4},{6,5},{7,6},{0,7},{9,8},{10,9},{11,1... | collective-permute-start | bytes 13832 | tf_op jit(solution)/shard_map/ppermute | solution.py:21
  (26 other events, 215.3 us)
where the time goes:
time: 565 us; the launch traced here: 555 us
  blocking collectives  154 us (27%)
  other arithmetic  143 us (25%)
  waiting for transfers between devices  115 us (20%)
  starting transfers between devices  94.7 us (17%)
  local copies, waits for them, and re-layouts  22.1 us (4%)
  matrix products  18.9 us (3%)
  between operations  6.16 us (1%)
    psum x3, blocking collectives, total_sum(): return lax.psum(value, ('lat', 'lon'))  117 us
    reduce_sum x24, other arithmetic, cells_to_rows(): jnp.sum(jnp.where(offsets[:, :, None] == columns, values[:, :, None], 0.0...  66.8 us
    ppermute x22, starting transfers between devices, with_halo(): lax.ppermute(lax.slice_in_dim(block, 0, width, axis=dim), axis, backward)  43.7 us
    ppermute x22, waiting for transfers between devices, with_halo(): lax.ppermute(lax.slice_in_dim(block, 0, width, axis=dim), axis, backward)  42.2 us
    reduce_sum x16, other arithmetic, rows_to_cells(): jnp.sum(jnp.where(offsets[:, :, None] == columns, rows[:, None, :], 0.0),...  41.2 us
    ppermute x22, waiting for transfers between devices, with_halo(): lax.ppermute(lax.slice_in_dim(block, block.shape[dim] - width, None, axis...  38.8 us
    all_to_all x2, blocking collectives, send_back(): lax.all_to_all(pack(to_rows(values)), ('lat', 'lon'), split_axis=0, conca...  36.8 us
    ppermute x22, starting transfers between devices, with_halo(): lax.ppermute(lax.slice_in_dim(block, block.shape[dim] - width, None, axis...  31.3 us
  transfers between devices with their start and end apart: 48, of which 26 were waited for; matrix products, arithmetic and copies ran while one was open for 5% of the time, Pallas kernels for 0%

commit v1 on v0

--- a/solution.py
+++ b/solution.py
@@ -66,7 +66,7 @@
 
 
 def total_sum(value):
-    return lax.psum(value, ("lat", "lon"))
+    return lax.psum(lax.psum(value, "lon"), "lat")
 
 
 def cells_to_rows(values, offsets):

time: 565 us -> 514 us (0.910)
  blocking collectives: 154 us -> 106 us
    psum x3 -> x6, blocking collectives: 117 us -> 69.5 us  [total_sum(): return lax.psum(lax.psum(value, 'lon'), 'lat')]
  transfers between devices with their start and end apart: 48 -> 48, of which waited for: 26 -> 25; matrix products, arithmetic and copies ran while one was open for 5% -> 6% of each run, Pallas kernels for 0% -> 0%
where the time goes in v1:
time: 514 us; the launch traced here: 504 us
  other arithmetic  143 us (28%)
  waiting for transfers between devices  114 us (22%)
  blocking collectives  106 us (21%)
  starting transfers between devices  92.4 us (18%)
  local copies, waits for them, and re-layouts  22.1 us (4%)
  matrix products  18.9 us (4%)
  between operations  5.92 us (1%)
    psum x6, blocking collectives, total_sum(): return lax.psum(lax.psum(value, 'lon'), 'lat')  69.5 us
    reduce_sum x24, other arithmetic, cells_to_rows(): jnp.sum(jnp.where(offsets[:, :, None] == columns, values[:, :, None], 0.0...  66.8 us
    ppermute x22, starting transfers between devices, with_halo(): lax.ppermute(lax.slice_in_dim(block, 0, width, axis=dim), axis, backward)  43.8 us
    ppermute x22, waiting for transfers between devices, with_halo(): lax.ppermute(lax.slice_in_dim(block, 0, width, axis=dim), axis, backward)  41.8 us
    reduce_sum x16, other arithmetic, rows_to_cells(): jnp.sum(jnp.where(offsets[:, :, None] == columns, rows[:, None, :], 0.0),...  41.2 us
    ppermute x22, waiting for transfers between devices, with_halo(): lax.ppermute(lax.slice_in_dim(block, block.shape[dim] - width, None, axis...  38.6 us
    all_to_all x2, blocking collectives, send_back(): lax.all_to_all(pack(to_rows(values)), ('lat', 'lon'), split_axis=0, conca...  36.8 us
    all_to_all x2, waiting for transfers between devices, on_device(): lax.all_to_all(jnp.dot(ownership, lst_of(lst_weights, image), precision=l...  30.8 us
  transfers between devices with their start and end apart: 48, of which 25 were waited for; matrix products, arithmetic and copies ran while one was open for 6% of the time, Pallas kernels for 0%

profile of v1, /device:TPU:0, one launch (start us, length us, event | category | flops | bytes accessed | tf_op | source)
XLA Modules:
  0.0 504.3 jit_solution(11760593519183698199)
XLA Ops:
  5.3 7.3 %all-to-all-start = ((s32[32,32,1]{1,2,0:T(1,128)}), s32[32,32,1]{1,2,0:T(1,128)S(1)}, u32[]{:S(2)}, u32[]{:S(2)}) async-start(s32[32,32,1]{1,2,0:T(1,128)} %sub.738), calls=%async_computation | async-start | bytes 32768 | tf_op jit(solution)/shard_map/all_to_all | solution.py:150
  13.7 22.9 %while.50 = (s32[]{:T(128)}, f32[8,64,128]{2,1,0:T(8,128)S(1)}, s32[8,64,128]{2,1,0:T(8,128)S(1)}, f32[8,64,128]{2,1,0:T(8,128)S(1)}, s32[]{:T(128)}) while((s32[]{:T(128)}, f32[8,64,128]{2,1,0:T(8,128)S(1)}, s32[8,64,128]{2,1,0:T(8,128)S(1)}, f32[8,64,128]{2,1,0:T(8,128)S(1)}, s32[]{:T(128)}) %tuple.124), condition=%wide.region_6.7_spmd, body=%wide.region_4.6_spmd.sunk | while | flops 3137538 | bytes 294985 | solution.py:90
  38.5 5.8 %all-to-all-start.1 = ((f32[32,32,128]{2,1,0:T(8,128)}), f32[32,32,128]{2,1,0:T(8,128)S(1)}, u32[]{:S(2)}, u32[]{:S(2)}) async-start(f32[32,32,128]{2,1,0:T(8,128)} %fusion.4), calls=%async_computation.1 | async-start | bytes 1048576 | tf_op jit(solution)/shard_map/all_to_all | solution.py:167
  60.8 5.1 %collective-permute-start = (f32[4,4,128]{2,1,0:T(4,128)S(1)}, f32[4,4,128]{2,1,0:T(4,128)S(1)}, u32[]{:S(2)}, u32[]{:S(2)}) collective-permute-start(f32[4,4,128]{2,1,0:T(4,128)S(1)} %get-tuple-element.208), channel_id=1, source_target_pairs={{0,8},{8,16},{16,24},{1,9},{9,17},{17,25},{2,10},{10,18},{18,26},{... | collective-permute-start | bytes 24584 | tf_op jit(solution)/shard_map/ppermute | solution.py:18
  67.5 4.0 collective-permute-done.1
  83.8 4.2 collective-permute-done.9
  90.8 4.4 collective-permute-done.10
  100.8 4.2 collective-permute-done.13
  117.2 4.2 collective-permute-done.17
  136.8 15.2 %all-to-all-done.2 = f32[32,32,128]{2,1,0:T(8,128)S(1)} async-done(((f32[32,32,128]{2,1,0:T(8,128)}), f32[32,32,128]{2,1,0:T(8,128)S(1)}, u32[]{:S(2)}, u32[]{:S(2)}) %all-to-all-start.2) | async-done | bytes 524320 | tf_op jit(solution)/shard_map/all_to_all | solution.py:179
  153.8 27.1 %while.51 = (s32[]{:T(128)}, f32[8,64,128]{2,1,0:T(8,128)S(1)}, s32[8,64,128]{2,1,0:T(8,128)S(1)}, f32[8,64,128]{2,1,0:T(8,128)}, s32[]{:T(128)}) while((s32[]{:T(128)}, f32[8,64,128]{2,1,0:T(8,128)S(1)}, s32[8,64,128]{2,1,0:T(8,128)S(1)}, f32[8,64,128]{2,1,0:T(8,128)}, s32[]{:T(128)}) %tuple.119), condition=%wide.region_12.13_spmd, body=%wide.region_10.12_spmd.sunk | while | flops 3137538 | bytes 294985 | solution.py:90
  181.7 27.3 %while.52 = (s32[]{:T(128)}, f32[8,64,128]{2,1,0:T(8,128)}, s32[8,64,128]{2,1,0:T(8,128)S(1)}, f32[8,64,128]{2,1,0:T(8,128)S(1)}, s32[]{:T(128)}) while((s32[]{:T(128)}, f32[8,64,128]{2,1,0:T(8,128)}, s32[8,64,128]{2,1,0:T(8,128)S(1)}, f32[8,64,128]{2,1,0:T(8,128)S(1)}, s32[]{:T(128)}) %tuple.125), condition=%wide.region_15.16_spmd, body=%wide.region_13.15_spmd.sunk | while | flops 3137538 | bytes 295493 | solution.py:90
  211.0 18.4 %all_to_all.54 = f32[32,32,128]{2,1,0:T(8,128)S(1)} all-to-all(f32[32,32,128]{2,1,0:T(8,128)S(1)} %fusion.2), channel_id=1, replica_groups=mesh['lat'=4,'lon'=8] {'lat','lon'}, dimensions={0} | all-to-all | bytes 1048576 | tf_op jit(solution)/shard_map/all_to_all | solution.py:167
  234.7 4.2 collective-permute-done.21
  241.9 4.0 collective-permute-done.22
  251.2 4.2 collective-permute-done.25
  258.2 4.0 collective-permute-done.26
  265.3 14.0 %all-reduce = (f32[]{:T(128)}, f32[]{:T(128)}) all-reduce(f32[]{:T(128)} %get-tuple-element.118, f32[]{:T(128)} %get-tuple-element.117), channel_id=1, replica_groups=mesh['lat'=4,'lon'=8] {'lon'}, use_global_device_ids=true, to_apply=%region_8.9 | all-reduce | flops 2 | bytes 16 | tf_op jit(solution)/shard_map/psum | solution.py:69
  279.2 9.0 %all-reduce.1 = (f32[]{:T(128)}, f32[]{:T(128)}) all-reduce(f32[]{:T(128)} %get-tuple-element.159, f32[]{:T(128)} %get-tuple-element.160), channel_id=1, replica_groups=mesh['lat'=4,'lon'=8] {'lat'}, use_global_device_ids=true, to_apply=%region_9.10 | all-reduce | flops 2 | bytes 16 | tf_op jit(solution)/shard_map/psum | solution.py:69
  290.2 12.4 %psum.60 = f32[]{:T(128)} all-reduce(f32[]{:T(128)} %multiply_reduce_fusion), channel_id=1, replica_groups=mesh['lat'=4,'lon'=8] {'lon'}, use_global_device_ids=true, to_apply=%region_20.21 | all-reduce | flops 1 | bytes 8 | tf_op jit(solution)/shard_map/psum | solution.py:69
  302.7 11.0 %psum.61 = f32[]{:T(128)} all-reduce(f32[]{:T(128)} %psum.60), channel_id=1, replica_groups=mesh['lat'=4,'lon'=8] {'lat'}, use_global_device_ids=true, to_apply=%region_21.22 | all-reduce | flops 1 | bytes 8 | tf_op jit(solution)/shard_map/psum | solution.py:69
  318.2 4.2 collective-permute-done.29
  334.8 4.2 collective-permute-done.33
  354.6 15.6 %all-to-all-done.4 = f32[32,32,128]{2,1,0:T(8,128)} async-done(((f32[32,32,128]{2,1,0:T(8,128)}), f32[32,32,128]{2,1,0:T(8,128)}, u32[]{:S(2)}, u32[]{:S(2)}) %all-to-all-start.4) | async-done | bytes 524320 | tf_op jit(solution)/shard_map/all_to_all | solution.py:179
  373.0 27.1 %while.53 = (s32[]{:T(128)}, f32[8,64,128]{2,1,0:T(8,128)S(1)}, s32[8,64,128]{2,1,0:T(8,128)S(1)}, f32[8,64,128]{2,1,0:T(8,128)}, s32[]{:T(128)}) while((s32[]{:T(128)}, f32[8,64,128]{2,1,0:T(8,128)S(1)}, s32[8,64,128]{2,1,0:T(8,128)S(1)}, f32[8,64,128]{2,1,0:T(8,128)}, s32[]{:T(128)}) %tuple.121), condition=%wide.region_24.25_spmd, body=%wide.region_22.24_spmd.sunk | while | flops 3137538 | bytes 294985 | solution.py:90
  400.1 22.9 %while.54 = (s32[]{:T(128)}, f32[8,64,128]{2,1,0:T(8,128)S(1)}, s32[8,64,128]{2,1,0:T(8,128)S(1)}, f32[8,64,128]{2,1,0:T(8,128)S(1)}, s32[]{:T(128)}) while((s32[]{:T(128)}, f32[8,64,128]{2,1,0:T(8,128)S(1)}, s32[8,64,128]{2,1,0:T(8,128)S(1)}, f32[8,64,128]{2,1,0:T(8,128)S(1)}, s32[]{:T(128)}) %tuple.123), condition=%wide.region_27.28_spmd, body=%wide.region_25.27_spmd.sunk | while | flops 3137538 | bytes 294985 | solution.py:90
  424.1 18.4 %all_to_all.55 = f32[32,32,128]{2,1,0:T(8,128)S(1)} all-to-all(f32[32,32,128]{2,1,0:T(8,128)S(1)} %fusion), channel_id=1, replica_groups=mesh['lat'=4,'lon'=8] {'lat','lon'}, dimensions={0} | all-to-all | bytes 1048576 | tf_op jit(solution)/shard_map/all_to_all | solution.py:167
  447.8 4.2 collective-permute-done.37
  454.8 4.3 collective-permute-done.38
  464.5 4.2 collective-permute-done.41
  478.3 14.1 %psum.62 = f32[]{:T(128)} all-reduce(f32[]{:T(128)} %fusion.267), channel_id=1, replica_groups=mesh['lat'=4,'lon'=8] {'lon'}, use_global_device_ids=true, to_apply=%region_29.30 | all-reduce | flops 1 | bytes 8 | tf_op jit(solution)/shard_map/psum | solution.py:69
  492.3 9.0 %psum.63 = f32[]{:T(128)} all-reduce(f32[]{:T(128)} %psum.62), channel_id=1, replica_groups=mesh['lat'=4,'lon'=8] {'lat'}, use_global_device_ids=true, to_apply=%region_30.31 | all-reduce | flops 1 | bytes 8 | tf_op jit(solution)/shard_map/psum | solution.py:69
  (386 shorter events, 283.4 us)
Async XLA Ops:
  5.3 33.1 %all-to-all-start = ((s32[32,32,1]{1,2,0:T(1,128)}), s32[32,32,1]{1,2,0:T(1,128)S(1)}, u32[]{:S(2)}, u32[]{:S(2)}) async-start(s32[32,32,1]{1,2,0:T(1,128)} %sub.738), calls=%async_computation | async-start | bytes 32768 | tf_op jit(solution)/shard_map/all_to_all | solution.py:150
  38.5 21.5 %all-to-all-start.1 = ((f32[32,32,128]{2,1,0:T(8,128)}), f32[32,32,128]{2,1,0:T(8,128)S(1)}, u32[]{:S(2)}, u32[]{:S(2)}) async-start(f32[32,32,128]{2,1,0:T(8,128)} %fusion.4), calls=%async_computation.1 | async-start | bytes 1048576 | tf_op jit(solution)/shard_map/all_to_all | solution.py:167
  44.4 9.4 %collective-permute-start.4 = (f32[8,4,128]{2,1,0:T(4,128)S(1)}, f32[8,4,128]{2,1,0:T(4,128)S(1)}, u32[]{:S(2)}, u32[]{:S(2)}) collective-permute-start(f32[8,4,128]{2,1,0:T(4,128)S(1)} %get-tuple-element.168), channel_id=1, source_target_pairs={{0,8},{8,16},{16,24},{1,9},{9,17},{17,25},{2,10},{10,18},{18,26},{... | collective-permute-start | bytes 49160 | tf_op jit(solution)/shard_map/ppermute | solution.py:18
  48.1 5.8 %collective-permute-start.5 = (f32[8,4,128]{2,1,0:T(4,128)S(1)}, f32[8,4,128]{2,1,0:T(4,128)S(1)}, u32[]{:S(2)}, u32[]{:S(2)}) collective-permute-start(f32[8,4,128]{2,1,0:T(4,128)S(1)} %get-tuple-element.169), channel_id=1, source_target_pairs={{8,0},{16,8},{24,16},{9,1},{17,9},{25,17},{10,2},{18,10},{26,18},{... | collective-permute-start | bytes 49160 | tf_op jit(solution)/shard_map/ppermute | solution.py:21
  54.1 13.1 %collective-permute-start.6 = (f32[8,72,4]{2,1,0:T(8,128)S(1)}, f32[8,72,4]{2,1,0:T(8,128)S(1)}, u32[]{:S(2)}, u32[]{:S(2)}) collective-permute-start(f32[8,72,4]{2,1,0:T(8,128)S(1)} %get-tuple-element.166), channel_id=1, source_target_pairs={{0,1},{1,2},{2,3},{3,4},{4,5},{5,6},{6,7},{7,0},{8,9},{9,10},{10,1... | collective-permute-start | bytes 27656 | tf_op jit(solution)/shard_map/ppermute | solution.py:18
  54.2 20.1 %collective-permute-start.7 = (f32[8,72,4]{2,1,0:T(8,128)S(1)}, f32[8,72,4]{2,1,0:T(8,128)}, u32[]{:S(2)}, u32[]{:S(2)}) collective-permute-start(f32[8,72,4]{2,1,0:T(8,128)S(1)} %get-tuple-element.167), channel_id=1, source_target_pairs={{1,0},{2,1},{3,2},{4,3},{5,4},{6,5},{7,6},{0,7},{9,8},{10,9},{11,1... | collective-permute-start | bytes 27656 | tf_op jit(solution)/shard_map/ppermute | solution.py:21
  60.8 6.7 %collective-permute-start = (f32[4,4,128]{2,1,0:T(4,128)S(1)}, f32[4,4,128]{2,1,0:T(4,128)S(1)}, u32[]{:S(2)}, u32[]{:S(2)}) collective-permute-start(f32[4,4,128]{2,1,0:T(4,128)S(1)} %get-tuple-element.208), channel_id=1, source_target_pairs={{0,8},{8,16},{16,24},{1,9},{9,17},{17,25},{2,10},{10,18},{18,26},{... | collective-permute-start | bytes 24584 | tf_op jit(solution)/shard_map/ppermute | solution.py:18
  71.6 6.2 %collective-permute-start.2 = (f32[4,72,4]{2,1,0:T(8,128)S(1)}, f32[4,72,4]{2,1,0:T(8,128)S(1)}, u32[]{:S(2)}, u32[]{:S(2)}) collective-permute-start(f32[4,72,4]{2,1,0:T(8,128)S(1)} %get-tuple-element.188), channel_id=1, source_target_pairs={{0,1},{1,2},{2,3},{3,4},{4,5},{5,6},{6,7},{7,0},{8,9},{9,10},{10,1... | collective-permute-start | bytes 13832 | tf_op jit(solution)/shard_map/ppermute | solution.py:18
  71.6 6.1 %collective-permute-start.3 = (f32[4,72,4]{2,1,0:T(8,128)S(1)}, f32[4,72,4]{2,1,0:T(8,128)S(1)}, u32[]{:S(2)}, u32[]{:S(2)}) collective-permute-start(f32[4,72,4]{2,1,0:T(8,128)S(1)} %get-tuple-element.189), channel_id=1, source_target_pairs={{1,0},{2,1},{3,2},{4,3},{5,4},{6,5},{7,6},{0,7},{9,8},{10,9},{11,1... | collective-permute-start | bytes 13832 | tf_op jit(solution)/shard_map/ppermute | solution.py:21
  82.4 5.5 %collective-permute-start.9 = (f32[4,4,128]{2,1,0:T(4,128)S(1)}, f32[4,4,128]{2,1,0:T(4,128)S(1)}, u32[]{:S(2)}, u32[]{:S(2)}) collective-permute-start(f32[4,4,128]{2,1,0:T(4,128)S(1)} %get-tuple-element.207), channel_id=1, source_target_pairs={{8,0},{16,8},{24,16},{9,1},{17,9},{25,17},{10,2},{18,10},{26,18},{... | collective-permute-start | bytes 24584 | tf_op jit(solution)/shard_map/ppermute | solution.py:21
  88.1 7.1 %collective-permute-start.10 = (f32[4,72,4]{2,1,0:T(8,128)S(1)}, f32[4,72,4]{2,1,0:T(8,128)S(1)}, u32[]{:S(2)}, u32[]{:S(2)}) collective-permute-start(f32[4,72,4]{2,1,0:T(8,128)S(1)} %get-tuple-element.186), channel_id=1, source_target_pairs={{0,1},{1,2},{2,3},{3,4},{4,5},{5,6},{6,7},{7,0},{8,9},{9,10},{10,1... | collective-permute-start | bytes 13832 | tf_op jit(solution)/shard_map/ppermute | solution.py:18
  88.1 7.0 %collective-permute-start.11 = (f32[4,72,4]{2,1,0:T(8,128)S(1)}, f32[4,72,4]{2,1,0:T(8,128)S(1)}, u32[]{:S(2)}, u32[]{:S(2)}) collective-permute-start(f32[4,72,4]{2,1,0:T(8,128)S(1)} %get-tuple-element.187), channel_id=1, source_target_pairs={{1,0},{2,1},{3,2},{4,3},{5,4},{6,5},{7,6},{0,7},{9,8},{10,9},{11,1... | collective-permute-start | bytes 13832 | tf_op jit(solution)/shard_map/ppermute | solution.py:21
  99.5 5.5 %collective-permute-start.13 = (f32[4,4,128]{2,1,0:T(4,128)S(1)}, f32[4,4,128]{2,1,0:T(4,128)S(1)}, u32[]{:S(2)}, u32[]{:S(2)}) collective-permute-start(f32[4,4,128]{2,1,0:T(4,128)S(1)} %get-tuple-element.205), channel_id=1, source_target_pairs={{8,0},{16,8},{24,16},{9,1},{17,9},{25,17},{10,2},{18,10},{26,18},{... | collective-permute-start | bytes 24584 | tf_op jit(solution)/shard_map/ppermute | solution.py:21
  105.2 6.4 %collective-permute-start.14 = (f32[4,72,4]{2,1,0:T(8,128)S(1)}, f32[4,72,4]{2,1,0:T(8,128)S(1)}, u32[]{:S(2)}, u32[]{:S(2)}) collective-permute-start(f32[4,72,4]{2,1,0:T(8,128)S(1)} %get-tuple-element.184), channel_id=1, source_target_pairs={{0,1},{1,2},{2,3},{3,4},{4,5},{5,6},{6,7},{7,0},{8,9},{9,10},{10,1... | collective-permute-start | bytes 13832 | tf_op jit(solution)/shard_map/ppermute | solution.py:18
  105.2 6.3 %collective-permute-start.15 = (f32[4,72,4]{2,1,0:T(8,128)S(1)}, f32[4,72,4]{2,1,0:T(8,128)S(1)}, u32[]{:S(2)}, u32[]{:S(2)}) collective-permute-start(f32[4,72,4]{2,1,0:T(8,128)S(1)} %get-tuple-element.185), channel_id=1, source_target_pairs={{1,0},{2,1},{3,2},{4,3},{5,4},{6,5},{7,6},{0,7},{9,8},{10,9},{11,1... | collective-permute-start | bytes 13832 | tf_op jit(solution)/shard_map/ppermute | solution.py:21
  115.9 5.5 %collective-permute-start.17 = (f32[4,4,128]{2,1,0:T(4,128)S(1)}, f32[4,4,128]{2,1,0:T(4,128)S(1)}, u32[]{:S(2)}, u32[]{:S(2)}) collective-permute-start(f32[4,4,128]{2,1,0:T(4,128)S(1)} %get-tuple-element.203), channel_id=1, source_target_pairs={{8,0},{16,8},{24,16},{9,1},{17,9},{25,17},{10,2},{18,10},{26,18},{... | collective-permute-start | bytes 24584 | tf_op jit(solution)/shard_map/ppermute | solution.py:21
  121.6 5.9 %collective-permute-start.18 = (f32[4,72,4]{2,1,0:T(8,128)S(1)}, f32[4,72,4]{2,1,0:T(8,128)S(1)}, u32[]{:S(2)}, u32[]{:S(2)}) collective-permute-start(f32[4,72,4]{2,1,0:T(8,128)S(1)} %get-tuple-element.182), channel_id=1, source_target_pairs={{0,1},{1,2},{2,3},{3,4},{4,5},{5,6},{6,7},{7,0},{8,9},{9,10},{10,1... | collective-permute-start | bytes 13832 | tf_op jit(solution)/shard_map/ppermute | solution.py:18
  121.6 5.9 %collective-permute-start.19 = (f32[4,72,4]{2,1,0:T(8,128)S(1)}, f32[4,72,4]{2,1,0:T(8,128)S(1)}, u32[]{:S(2)}, u32[]{:S(2)}) collective-permute-start(f32[4,72,4]{2,1,0:T(8,128)S(1)} %get-tuple-element.183), channel_id=1, source_target_pairs={{1,0},{2,1},{3,2},{4,3},{5,4},{6,5},{7,6},{0,7},{9,8},{10,9},{11,1... | collective-permute-start | bytes 13832 | tf_op jit(solution)/shard_map/ppermute | solution.py:21
  133.6 18.5 %all-to-all-start.2 = ((f32[32,32,128]{2,1,0:T(8,128)}), f32[32,32,128]{2,1,0:T(8,128)S(1)}, u32[]{:S(2)}, u32[]{:S(2)}) async-start(f32[32,32,128]{2,1,0:T(8,128)} %fusion.18), calls=%async_computation.2 | async-start | bytes 1048576 | tf_op jit(solution)/shard_map/all_to_all | solution.py:179
  233.4 5.5 %collective-permute-start.21 = (f32[4,4,128]{2,1,0:T(4,128)S(1)}, f32[4,4,128]{2,1,0:T(4,128)S(1)}, u32[]{:S(2)}, u32[]{:S(2)}) collective-permute-start(f32[4,4,128]{2,1,0:T(4,128)S(1)} %get-tuple-element.201), channel_id=1, source_target_pairs={{8,0},{16,8},{24,16},{9,1},{17,9},{25,17},{10,2},{18,10},{26,18},{... | collective-permute-start | bytes 24584 | tf_op jit(solution)/shard_map/ppermute | solution.py:21
  239.0 6.8 %collective-permute-start.22 = (f32[4,72,4]{2,1,0:T(8,128)S(1)}, f32[4,72,4]{2,1,0:T(8,128)S(1)}, u32[]{:S(2)}, u32[]{:S(2)}) collective-permute-start(f32[4,72,4]{2,1,0:T(8,128)S(1)} %get-tuple-element.180), channel_id=1, source_target_pairs={{0,1},{1,2},{2,3},{3,4},{4,5},{5,6},{6,7},{7,0},{8,9},{9,10},{10,1... | collective-permute-start | bytes 13832 | tf_op jit(solution)/shard_map/ppermute | solution.py:18
  239.1 6.8 %collective-permute-start.23 = (f32[4,72,4]{2,1,0:T(8,128)S(1)}, f32[4,72,4]{2,1,0:T(8,128)S(1)}, u32[]{:S(2)}, u32[]{:S(2)}) collective-permute-start(f32[4,72,4]{2,1,0:T(8,128)S(1)} %get-tuple-element.181), channel_id=1, source_target_pairs={{1,0},{2,1},{3,2},{4,3},{5,4},{6,5},{7,6},{0,7},{9,8},{10,9},{11,1... | collective-permute-start | bytes 13832 | tf_op jit(solution)/shard_map/ppermute | solution.py:21
  249.9 5.5 %collective-permute-start.25 = (f32[4,4,128]{2,1,0:T(4,128)S(1)}, f32[4,4,128]{2,1,0:T(4,128)S(1)}, u32[]{:S(2)}, u32[]{:S(2)}) collective-permute-start(f32[4,4,128]{2,1,0:T(4,128)S(1)} %get-tuple-element.199), channel_id=1, source_target_pairs={{8,0},{16,8},{24,16},{9,1},{17,9},{25,17},{10,2},{18,10},{26,18},{... | collective-permute-start | bytes 24584 | tf_op jit(solution)/shard_map/ppermute | solution.py:21
  255.5 6.7 %collective-permute-start.26 = (f32[4,72,4]{2,1,0:T(8,128)S(1)}, f32[4,72,4]{2,1,0:T(8,128)S(1)}, u32[]{:S(2)}, u32[]{:S(2)}) collective-permute-start(f32[4,72,4]{2,1,0:T(8,128)S(1)} %get-tuple-element.178), channel_id=1, source_target_pairs={{0,1},{1,2},{2,3},{3,4},{4,5},{5,6},{6,7},{7,0},{8,9},{9,10},{10,1... | collective-permute-start | bytes 13832 | tf_op jit(solution)/shard_map/ppermute | solution.py:18
  255.6 6.6 %collective-permute-start.27 = (f32[4,72,4]{2,1,0:T(8,128)S(1)}, f32[4,72,4]{2,1,0:T(8,128)S(1)}, u32[]{:S(2)}, u32[]{:S(2)}) collective-permute-start(f32[4,72,4]{2,1,0:T(8,128)S(1)} %get-tuple-element.179), channel_id=1, source_target_pairs={{1,0},{2,1},{3,2},{4,3},{5,4},{6,5},{7,6},{0,7},{9,8},{10,9},{11,1... | collective-permute-start | bytes 13832 | tf_op jit(solution)/shard_map/ppermute | solution.py:21
  322.5 6.6 %collective-permute-start.30 = (f32[4,72,4]{2,1,0:T(8,128)S(1)}, f32[4,72,4]{2,1,0:T(8,128)S(1)}, u32[]{:S(2)}, u32[]{:S(2)}) collective-permute-start(f32[4,72,4]{2,1,0:T(8,128)S(1)} %get-tuple-element.176), channel_id=1, source_target_pairs={{0,1},{1,2},{2,3},{3,4},{4,5},{5,6},{6,7},{7,0},{8,9},{9,10},{10,1... | collective-permute-start | bytes 13832 | tf_op jit(solution)/shard_map/ppermute | solution.py:18
  322.6 6.5 %collective-permute-start.31 = (f32[4,72,4]{2,1,0:T(8,128)S(1)}, f32[4,72,4]{2,1,0:T(8,128)S(1)}, u32[]{:S(2)}, u32[]{:S(2)}) collective-permute-start(f32[4,72,4]{2,1,0:T(8,128)S(1)} %get-tuple-element.177), channel_id=1, source_target_pairs={{1,0},{2,1},{3,2},{4,3},{5,4},{6,5},{7,6},{0,7},{9,8},{10,9},{11,1... | collective-permute-start | bytes 13832 | tf_op jit(solution)/shard_map/ppermute | solution.py:21
  350.7 19.5 %all-to-all-start.4 = ((f32[32,32,128]{2,1,0:T(8,128)}), f32[32,32,128]{2,1,0:T(8,128)}, u32[]{:S(2)}, u32[]{:S(2)}) async-start(f32[32,32,128]{2,1,0:T(8,128)} %fusion.16), calls=%async_computation.4 | async-start | bytes 1048576 | tf_op jit(solution)/shard_map/all_to_all | solution.py:179
  452.1 7.0 %collective-permute-start.38 = (f32[4,72,4]{2,1,0:T(8,128)S(1)}, f32[4,72,4]{2,1,0:T(8,128)S(1)}, u32[]{:S(2)}, u32[]{:S(2)}) collective-permute-start(f32[4,72,4]{2,1,0:T(8,128)S(1)} %get-tuple-element.172), channel_id=1, source_target_pairs={{0,1},{1,2},{2,3},{3,4},{4,5},{5,6},{6,7},{7,0},{8,9},{9,10},{10,1... | collective-permute-start | bytes 13832 | tf_op jit(solution)/shard_map/ppermute | solution.py:18
  452.2 6.9 %collective-permute-start.39 = (f32[4,72,4]{2,1,0:T(8,128)S(1)}, f32[4,72,4]{2,1,0:T(8,128)S(1)}, u32[]{:S(2)}, u32[]{:S(2)}) collective-permute-start(f32[4,72,4]{2,1,0:T(8,128)S(1)} %get-tuple-element.173), channel_id=1, source_target_pairs={{1,0},{2,1},{3,2},{4,3},{5,4},{6,5},{7,6},{0,7},{9,8},{10,9},{11,1... | collective-permute-start | bytes 13832 | tf_op jit(solution)/shard_map/ppermute | solution.py:21
  468.8 6.5 %collective-permute-start.42 = (f32[4,72,4]{2,1,0:T(8,128)S(1)}, f32[4,72,4]{2,1,0:T(8,128)S(1)}, u32[]{:S(2)}, u32[]{:S(2)}) collective-permute-start(f32[4,72,4]{2,1,0:T(8,128)S(1)} %get-tuple-element.170), channel_id=1, source_target_pairs={{0,1},{1,2},{2,3},{3,4},{4,5},{5,6},{6,7},{7,0},{8,9},{9,10},{10,1... | collective-permute-start | bytes 13832 | tf_op jit(solution)/shard_map/ppermute | solution.py:18
  468.8 6.4 %collective-permute-start.43 = (f32[4,72,4]{2,1,0:T(8,128)S(1)}, f32[4,72,4]{2,1,0:T(8,128)S(1)}, u32[]{:S(2)}, u32[]{:S(2)}) collective-permute-start(f32[4,72,4]{2,1,0:T(8,128)S(1)} %get-tuple-element.171), channel_id=1, source_target_pairs={{1,0},{2,1},{3,2},{4,3},{5,4},{6,5},{7,6},{0,7},{9,8},{10,9},{11,1... | collective-permute-start | bytes 13832 | tf_op jit(solution)/shard_map/ppermute | solution.py:21
  (26 other events, 182.7 us)
